TPU v7x, 256 devices: a whole 4x4x8 slice. The times are simulated.
256 devices in a mesh: seq: 32 (over x, z_lo, core), dp: 8 (over z_hi, y).
Axes of the slice: x: 4, y: 4, z: 8 (z_hi: 2, z_lo: 4; z = z_hi * 4 + z_lo), core: 2. Of those that a mesh axis runs over, the one named last changes fastest.
Arguments:
- tokens: bfloat16 [8, 16384, 1536], P('dp', 'seq'), may hold values from -6 to 6
- cotangent: bfloat16 [8, 16384, 1536], P('dp', 'seq'), may hold values from -6 to 6
- conv_weight: float32 [3, 1536], replicated, may hold values from -3.5 to 3.5
- gate_weight: bfloat16 [1536, 1536], P('seq'), may hold values from -0.15625 to 0.15625
- leading_block_factor: bfloat16 [128, 128, 128], P('seq'), may hold values from -0.5 to 0.5
- trailing_block_factor: bfloat16 [128, 128, 128], P('seq'), may hold values from -0.5 to 0.5
Outputs:
- mixed: bfloat16 [8, 16384, 1536], P('dp', 'seq')
- grad_tokens: bfloat16 [8, 16384, 1536], P('dp', 'seq')
- grad_conv: float32 [3, 1536], replicated
- grad_gate: float32 [1536, 1536], P('seq')
- grad_first: float32 [128, 128, 128], P('seq')
- trailing_factor_gradient: float32 [128, 128, 128], P('seq')
All inputs are finite; a program needn't handle non-finite values.
Results may differ from a plain program's by a relative error of at most 0.0067.
Values may be sent and summed in bfloat16 or wider, within the bound.
No kernel may reach another device: no remote copies, remote signals or barrier semaphores. Data moves between devices by JAX's collectives and lax.ppermute only.
A program may use at most 128 MiB of HBM per device.

v0:
```python
import jax
import jax.numpy as jnp
from jax import lax
from jax.sharding import PartitionSpec as P


def with_halo(array, sides, width):
    for axis, dim in sides:
        count, length = (lax.axis_size(axis), array.shape[dim])
        up = [(i, (i + 1) % count) for i in range(count - 1)]
        down = [(j, i) for i, j in up]
        last = lax.slice_in_dim(array, length - width, length, axis=dim)
        first = lax.slice_in_dim(array, 0, width, axis=dim)
        before = lax.ppermute(last, axis, up)
        after = lax.ppermute(first, axis, down)
        array = jnp.concatenate([before, array, after], axis=dim)
    return array


def extend(values):
    return with_halo(values, (("seq", 0),), 1)


def regroup(values):
    return lax.all_to_all(values, "seq", split_axis=0, concat_axis=1, tiled=True)


def shards(
    tokens, cotangent, conv_weight, gate_weight, leading_block_factor, trailing_block_factor
):
    features = tokens[0]
    grad_out = cotangent[0]
    tok_rows = features.shape[0]
    feat_width = features.shape[1]
    local_blocks = leading_block_factor.shape[0]
    block_size = leading_block_factor.shape[1]
    feat_wide = features.astype(jnp.float32)
    pad_feat = extend(features).astype(jnp.float32)
    conv_in = (
        conv_weight[0] * pad_feat[:-2] + conv_weight[1] * feat_wide + conv_weight[2] * pad_feat[2:]
    ).astype(jnp.bfloat16)
    convolution_block_list = conv_in.reshape(local_blocks, block_size, feat_width)
    leading_output = jnp.einsum(
        "shz,szy->hsy",
        leading_block_factor,
        convolution_block_list,
        preferred_element_type=jnp.float32,
    ).astype(jnp.bfloat16)
    column_layout = regroup(leading_output)
    trailing_output = jnp.einsum(
        "vpn,vnu->pvu", trailing_block_factor, column_layout, preferred_element_type=jnp.float32
    ).astype(jnp.bfloat16)
    monarch = regroup(trailing_output).reshape(tok_rows, feat_width)
    whole_gate = lax.all_gather(gate_weight, "seq", axis=0, tiled=True)
    gate_act = jnp.dot(features, whole_gate, preferred_element_type=jnp.float32)
    mon_wide = monarch.astype(jnp.float32)
    grad_wide = grad_out.astype(jnp.float32)
    mixed = (mon_wide * gate_act).astype(jnp.bfloat16)
    d_monarch = (grad_wide * gate_act).astype(jnp.bfloat16)
    d_gate = (grad_wide * mon_wide).astype(jnp.bfloat16)
    second_factor_delta = lax.all_to_all(
        d_monarch.reshape(local_blocks, block_size, feat_width),
        "seq",
        split_axis=1,
        concat_axis=0,
        tiled=True,
    )
    d_inner = jnp.einsum(
        "ica,cid->aid",
        trailing_block_factor,
        second_factor_delta,
        preferred_element_type=jnp.float32,
    ).astype(jnp.bfloat16)
    trailing_factor_gradient = jnp.einsum(
        "wxn,xon->xwo", second_factor_delta, column_layout, preferred_element_type=jnp.float32
    )
    d_first = regroup(d_inner)
    d_conv = (
        jnp.einsum(
            "aib,aid->abd", leading_block_factor, d_first, preferred_element_type=jnp.float32
        )
        .astype(jnp.bfloat16)
        .reshape(tok_rows, feat_width)
    )
    grad_first = jnp.einsum(
        "aid,abd->aib", d_first, convolution_block_list, preferred_element_type=jnp.float32
    )
    d_convw = d_conv.astype(jnp.float32)
    conv_part = jnp.stack(
        [
            jnp.sum(d_convw * pad_feat[:-2], axis=0),
            jnp.sum(d_convw * feat_wide, axis=0),
            jnp.sum(d_convw * pad_feat[2:], axis=0),
        ]
    )
    pad_grad = extend(d_conv).astype(jnp.float32)
    conv_back = (
        conv_weight[0] * pad_grad[2:] + conv_weight[1] * d_convw + conv_weight[2] * pad_grad[:-2]
    )
    gate_back = lax.dot_general(
        d_gate, whole_gate, (((1,), (1,)), ((), ())), preferred_element_type=jnp.float32
    )
    grad_tokens = (conv_back + gate_back).astype(jnp.bfloat16)
    weight_part = lax.psum_scatter(
        lax.dot_general(
            features, d_gate, (((0,), (0,)), ((), ())), preferred_element_type=jnp.float32
        ),
        "seq",
        scatter_dimension=0,
        tiled=True,
    )
    grad_first, trailing_factor_gradient = lax.psum((grad_first, trailing_factor_gradient), "dp")
    grad_gate = lax.psum(weight_part, "dp")
    grad_conv = lax.psum(conv_part, ("seq", "dp"))
    return (
        mixed[None],
        grad_tokens[None],
        grad_conv,
        grad_gate,
        grad_first,
        trailing_factor_gradient,
    )


def solution(mesh):
    return jax.shard_map(
        shards,
        mesh=mesh,
        in_specs=(
            P("dp", "seq", None),
            P("dp", "seq", None),
            P(),
            P("seq", None),
            P("seq", None, None),
            P("seq", None, None),
        ),
        out_specs=(
            P("dp", "seq", None),
            P("dp", "seq", None),
            P(),
            P("seq", None),
            P("seq", None, None),
            P("seq", None, None),
        ),
        check_vma=False,
    )
```

profile of v0, /device:TPU:2, one launch (start us, length us, event | category | flops | bytes accessed | tf_op | source)
XLA Modules:
  0.0 599.1 jit_solution(1992488106284117112)
XLA Ops:
  7.9 68.7 %all-gather.2.cloned.1.call-done = bf16[1536,1536]{1,0:T(8,128)(2,1)} async-done(((bf16[48,1536]{1,0:T(8,128)(2,1)}), bf16[1536,1536]{1,0:T(8,128)(2,1)}) %all-gather.2.cloned.1.call-update) | async-done | bytes 4718608 | tf_op jit(solution)/shard_map/all_gather | solution.py:54
  76.6 7.6 %fusion.2 = (bf16[512,1536]{1,0:T(8,128)(2,1)S(1)}, f32[512,1536]{1,0:T(8,128)}) fusion(bf16[1,512,1536]{2,1,0:T(8,128)(2,1)} %param.7, bf16[1536,1536]{1,0:T(8,128)(2,1)} %all-gather.2.cloned.1.call-done, bf16[1,512,1536]{2,1,0:T(8,128)(2,1)} %param.6), kind=kOutput, calls=%fused_computation.9 | convolution fusion | flops 2418278400 | bytes 12582912 | tf_op jit(solution)/shard_map/dot_general | solution.py:55
  85.4 42.4 %all_to_all.63 = bf16[4,128,1536]{2,0,1:T(4,128)(2,1)S(1)} all-to-all(bf16[4,128,1536]{2,0,1:T(4,128)(2,1)S(1)} %copy.58), channel_id=1, replica_groups=mesh['seq'=32,'dp'=8] {'seq'}, dimensions={1} | all-to-all | bytes 3145728 | tf_op jit(solution)/shard_map/all_to_all | solution.py:61
  130.4 2.5 copy.61
  132.9 7.2 %all-to-all-start.3 = ((bf16[128,4,1536]{2,1,0:T(4,128)(2,1)}), bf16[128,4,1536]{2,1,0:T(4,128)(2,1)}, u32[]{:S(2)}, u32[]{:S(2)}) async-start(bf16[128,4,1536]{2,1,0:T(4,128)(2,1)} %copy.61), calls=%async_computation.3 | async-start | bytes 3145728 | tf_op jit(solution)/shard_map/all_to_all | solution.py:25
  143.0 6.2 %collective-permute-start.1 = (bf16[1,1536]{1,0:T(2,128)(2,1)S(1)}, bf16[1,1536]{1,0:T(2,128)(2,1)S(1)}, u32[]{:S(2)}, u32[]{:S(2)}) collective-permute-start(bf16[1,1536]{1,0:T(2,128)(2,1)S(1)} %get-tuple-element.42), channel_id=1, source_target_pairs={{8,0},{16,8},{24,16},{32,24},{40,32},{48,40},{56,48},{64,56},{72,6... | collective-permute-start | bytes 9224 | tf_op jit(solution)/shard_map/ppermute | solution.py:15
  149.3 20.2 %collective-permute-done = bf16[1,1536]{1,0:T(2,128)(2,1)S(1)} collective-permute-done((bf16[1,1536]{1,0:T(2,128)(2,1)S(1)}, bf16[1,1536]{1,0:T(2,128)(2,1)S(1)}, u32[]{:S(2)}, u32[]{:S(2)}) %collective-permute-start) | collective-permute-done | bytes 3104 | tf_op jit(solution)/shard_map/ppermute | solution.py:14
  171.4 5.5 all-to-all-done.3
  176.9 3.1 copy.62
  180.0 3.7 all_to_all.58
  183.7 2.6 fusion.9
  191.1 43.9 %all_to_all.64 = bf16[128,4,1536]{2,1,0:T(4,128)(2,1)S(1)} all-to-all(bf16[128,4,1536]{2,1,0:T(4,128)(2,1)S(1)} %copy.53), channel_id=1, replica_groups=mesh['seq'=32,'dp'=8] {'seq'}, dimensions={0} | all-to-all | bytes 3145728 | tf_op jit(solution)/shard_map/all_to_all | solution.py:25
  239.2 42.8 %all_to_all.65 = bf16[128,4,1536]{2,1,0:T(4,128)(2,1)S(1)} all-to-all(bf16[128,4,1536]{2,1,0:T(4,128)(2,1)S(1)} %copy.56), channel_id=1, replica_groups=mesh['seq'=32,'dp'=8] {'seq'}, dimensions={0} | all-to-all | bytes 3145728 | tf_op jit(solution)/shard_map/all_to_all | solution.py:25
  282.7 2.3 reshape.55
  284.9 9.1 %convolution_bitcast_fusion = f32[1536,1536]{0,1:T(8,128)} fusion(f32[1,512,1536]{2,1,0:T(8,128)} %reshape.55, bf16[1,512,1536]{2,1,0:T(8,128)(2,1)} %param.7, bf16[1,512,1536]{2,1,0:T(8,128)(2,1)} %param.6), kind=kOutput, calls=%fused_computation | convolution fusion | flops 2418278400 | bytes 15728640 | tf_op jit(solution)/shard_map/dot_general | solution.py:105
  294.1 9.6 %copy.70 = f32[1536,1536]{1,0:T(8,128)} copy(f32[1536,1536]{0,1:T(8,128)} %convolution_bitcast_fusion) | data formatting | bytes 18874368
  304.6 3.6 collective-permute-start.2
  308.2 4.7 collective-permute-start.3
  312.9 3.2 fusion.28
  316.1 75.9 %psum.28 = f32[3,1536]{1,0:T(4,128)} all-reduce(f32[3,1536]{1,0:T(4,128)S(1)} %pad_maximum_fusion), channel_id=1, replica_groups=mesh['seq'=32,'dp'=8] {'seq','dp'}, use_global_device_ids=true, to_apply=%region_3.0 | all-reduce | flops 4608 | bytes 36864 | tf_op jit(solution)/shard_map/psum | solution.py:114
  392.0 3.7 maximum_convert_fusion.1
  399.3 50.2 %reduce-scatter.4.cloned.1.call-done = f32[48,1536]{1,0:T(8,128)} async-done(((f32[1536,1536]{1,0:T(8,128)}), f32[48,1536]{1,0:T(8,128)}) %reduce-scatter.4.cloned.1.call-update) | async-done | bytes 294928
  451.7 9.8 %fusion.14 = bf16[1,512,1536]{2,1,0:T(8,128)(2,1)} fusion(bf16[1536,1536]{1,0:T(8,128)(2,1)} %all-gather.2.cloned.1.call-done, f32[514,1536]{1,0:T(8,128)} %maximum_convert_fusion.1, bf16[512,1536]{1,0:T(8,128)(2,1)S(1)} %bitcast.78, f32[512,1536]{1,0:T(8,128)} %reshape.52, bf16[1,512,1536]{2,1,0:T(8,128)(2,1)} %param.7, f32[1536]{0:T(1024)S(1)} %get-tuple-element.33, ...), kind=kOutput, calls=%fused_computation.31 | convolution fusion | flops 2424569856 | bytes 18892800 | tf_op jit(solution)/shard_map/dot_general | solution.py:100
  463.0 125.0 %all-reduce.3.cloned.1.call-done = (f32[48,1536]{0,1:T(8,128)}, f32[4,128,128]{2,1,0:T(8,128)}, f32[4,128,128]{2,1,0:T(8,128)}) async-done(((f32[48,1536]{0,1:T(8,128)}, f32[4,128,128]{2,1,0:T(8,128)}, f32[4,128,128]{2,1,0:T(8,128)}), (f32[48,1536]{0,1:T(8,128)}, f32[4,128,128]{2,1,0:T(8,128)}, f32[4,128,128]{2,1,0:T(8,128)})) %all-reduce.3.cloned.1.call-update) | async-done | bytes 819216 | tf_op jit(solution)/shard_map/psum | solution.py:113
  (66 shorter events, 31.7 us)
Async XLA Ops:
  7.2 176.5 %copy-start = (bf16[4,128,128]{2,1,0:T(8,128)(2,1)S(1)}, bf16[4,128,128]{2,1,0:T(8,128)(2,1)}, u32[]{:S(2)}) copy-start(bf16[4,128,128]{2,1,0:T(8,128)(2,1)} %param.10) | copy-start | bytes 393220
  7.2 69.4 %all-gather.2.cloned.1.call-start = ((), (), s32[]{:S(2)}) async-start(), calls=%async_computation.5 | async-start | bytes 4866048 | tf_op jit(solution)/shard_map/all_gather | solution.py:54
  127.8 1.9 copy-start.12
  128.5 1.1 copy-start.7
  132.9 16.3 %copy-start.14 = (f32[3,1536]{1,0:T(4,128)S(1)}, f32[3,1536]{1,0:T(4,128)}, u32[]{:S(2)}) copy-start(f32[3,1536]{1,0:T(4,128)} %param.8) | copy-start | bytes 55300
  132.9 44.0 %all-to-all-start.3 = ((bf16[128,4,1536]{2,1,0:T(4,128)(2,1)}), bf16[128,4,1536]{2,1,0:T(4,128)(2,1)}, u32[]{:S(2)}, u32[]{:S(2)}) async-start(bf16[128,4,1536]{2,1,0:T(4,128)(2,1)} %copy.61), calls=%async_computation.3 | async-start | bytes 3145728 | tf_op jit(solution)/shard_map/all_to_all | solution.py:25
  140.1 309.4 %reduce-scatter.4.cloned.1.call-start = ((), (), s32[]{:S(2)}) async-start(), calls=%async_computation.6 | async-start | bytes 9732096
  140.9 28.6 %collective-permute-start = (bf16[1,1536]{1,0:T(2,128)(2,1)S(1)}, bf16[1,1536]{1,0:T(2,128)(2,1)S(1)}, u32[]{:S(2)}, u32[]{:S(2)}) collective-permute-start(bf16[1,1536]{1,0:T(2,128)(2,1)S(1)} %get-tuple-element.41), channel_id=1, source_target_pairs={{0,8},{8,16},{16,24},{24,32},{32,40},{40,48},{48,56},{56,64},{64,7... | collective-permute-start | bytes 9224 | tf_op jit(solution)/shard_map/ppermute | solution.py:14
  143.0 26.5 %collective-permute-start.1 = (bf16[1,1536]{1,0:T(2,128)(2,1)S(1)}, bf16[1,1536]{1,0:T(2,128)(2,1)S(1)}, u32[]{:S(2)}, u32[]{:S(2)}) collective-permute-start(bf16[1,1536]{1,0:T(2,128)(2,1)S(1)} %get-tuple-element.42), channel_id=1, source_target_pairs={{8,0},{16,8},{24,16},{32,24},{40,32},{48,40},{56,48},{64,56},{72,6... | collective-permute-start | bytes 9224 | tf_op jit(solution)/shard_map/ppermute | solution.py:15
  183.7 2.6 copy-start.2
  186.3 1.6 copy-start.3
  187.9 1.2 copy-start.5
  235.8 1.2 copy-start.9
  303.8 284.3 %all-reduce.3.cloned.1.call-start = ((), (), s32[]{:S(2)}) async-start(), calls=%async_computation.7 | async-start | bytes 2621440 | tf_op jit(solution)/shard_map/psum | solution.py:113
  304.6 87.4 %collective-permute-start.2 = (bf16[1,1536]{1,0:T(2,128)(2,1)S(1)}, bf16[1,1536]{1,0:T(2,128)(2,1)S(1)}, u32[]{:S(2)}, u32[]{:S(2)}) collective-permute-start(bf16[1,1536]{1,0:T(2,128)(2,1)S(1)} %get-tuple-element.39), channel_id=1, source_target_pairs={{0,8},{8,16},{16,24},{24,32},{32,40},{40,48},{48,56},{56,64},{64,7... | collective-permute-start | bytes 9224 | tf_op jit(solution)/shard_map/ppermute | solution.py:14
  308.2 83.8 %collective-permute-start.3 = (bf16[1,1536]{1,0:T(2,128)(2,1)S(1)}, bf16[1,1536]{1,0:T(2,128)(2,1)S(1)}, u32[]{:S(2)}, u32[]{:S(2)}) collective-permute-start(bf16[1,1536]{1,0:T(2,128)(2,1)S(1)} %get-tuple-element.40), channel_id=1, source_target_pairs={{8,0},{16,8},{24,16},{32,24},{40,32},{48,40},{56,48},{64,56},{72,6... | collective-permute-start | bytes 9224 | tf_op jit(solution)/shard_map/ppermute | solution.py:15
  392.0 3.8 copy-start.8
  392.0 3.8 copy-start.10
  399.3 52.4 %copy-start.4 = (bf16[4,1536,128]{1,2,0:T(8,128)(2,1)S(1)}, bf16[4,1536,128]{1,2,0:T(8,128)(2,1)}, u32[]{:S(2)}) copy-start(bf16[4,1536,128]{1,2,0:T(8,128)(2,1)} %copy-done.3) | copy-start | bytes 4718596
  451.6 9.8 %copy-start.6 = (f32[512,1536]{1,0:T(8,128)S(1)}, f32[512,1536]{1,0:T(8,128)}, u32[]{:S(2)}) copy-start(f32[512,1536]{1,0:T(8,128)} %reshape.52) | copy-start | bytes 9437188
  451.7 9.8 %copy-start.11 = (f32[512,1536]{1,0:T(8,128)S(1)}, f32[512,1536]{1,0:T(8,128)}, u32[]{:S(2)}) copy-start(f32[512,1536]{1,0:T(8,128)} %get-tuple-element.44) | copy-start | bytes 9437188
  461.5 131.1 %copy-start.1 = (bf16[4,128,128]{2,1,0:T(8,128)(2,1)S(1)}, bf16[4,128,128]{2,1,0:T(8,128)(2,1)}, u32[]{:S(2)}) copy-start(bf16[4,128,128]{2,1,0:T(8,128)(2,1)} %param.10) | copy-start | bytes 393220
  588.0 3.8 copy-start.13
Sparse Core Ops, SparseCore 0:
  9.9 66.6 all-gather.1
  303.9 145.5 reduce-scatter.3
  452.9 135.0 all-reduce.2
where the time goes:
time: 600 us; the launch traced here: 599 us
  waiting for transfers between devices  270 us (45%)
  blocking collectives  205 us (34%)
  local copies, waits for them, and re-layouts  41 us (7%)
  matrix products  35.8 us (6%)
  starting transfers between devices  23.9 us (4%)
  between operations  14 us (2%)
  other arithmetic  9.23 us (2%)
    psum x1, waiting for transfers between devices, shards(): grad_gate = lax.psum(weight_part, 'dp')  125 us
    all_to_all x2, blocking collectives, regroup(): lax.all_to_all(values, 'seq', split_axis=0, concat_axis=1, tiled=True)  86.7 us
    psum x1, blocking collectives, shards(): grad_conv = lax.psum(conv_part, ('seq', 'dp'))  75.9 us
    all_gather x1, waiting for transfers between devices, shards(): whole_gate = lax.all_gather(gate_weight, 'seq', axis=0, tiled=True)  68.7 us
    unnamed x4, waiting for transfers between devices  50.9 us
    all_to_all x1, blocking collectives, shards(): lax.all_to_all(d_monarch.reshape(local_blocks, block_size, feat_width), '...  42.4 us
    ppermute x2, waiting for transfers between devices, with_halo(): before = lax.ppermute(last, axis, up)  20.2 us
    unnamed x35, local copies, waits for them, and re-layouts  19.9 us
  transfers between devices with their start and end apart: 8, of which 5 were waited for; matrix products, arithmetic and copies ran while one was open for 4% of the time, Pallas kernels for 0%

commit v1 on v0

--- a/solution.py
+++ b/solution.py
@@ -2,6 +2,7 @@
 import jax.numpy as jnp
 from jax import lax
 from jax.sharding import PartitionSpec as P
+from jax.lax import psum
 
 
 def with_halo(array, sides, width):
@@ -111,7 +112,8 @@
     )
     grad_first, trailing_factor_gradient = lax.psum((grad_first, trailing_factor_gradient), "dp")
     grad_gate = lax.psum(weight_part, "dp")
-    grad_conv = lax.psum(conv_part, ("seq", "dp"))
+    parts_out = psum(conv_part, "seq")
+    grad_conv = psum(parts_out, "dp")
     return (
         mixed[None],
         grad_tokens[None],

time: 600 us -> 637 us (1.062)
  blocking collectives: 205 us -> 297 us
  waiting for transfers between devices: 270 us -> 215 us
    psum x1 -> x2, blocking collectives: 75.9 us -> 168 us  [the longest x1 115 us: shards(): parts_out = psum(conv_part, 'seq')]
    unnamed x4, waiting for transfers between devices: 50.9 us -> 0.72 us
  transfers between devices with their start and end apart: 8 -> 8, of which waited for: 5 -> 4; matrix products, arithmetic and copies ran while one was open for 4% -> 4% of each run, Pallas kernels for 0% -> 0%
where the time goes in v1:
time: 637 us; the launch traced here: 636 us
  blocking collectives  297 us (47%)
  waiting for transfers between devices  215 us (34%)
  local copies, waits for them, and re-layouts  41 us (6%)
  matrix products  35.8 us (6%)
  starting transfers between devices  23.9 us (4%)
  between operations  14 us (2%)
  other arithmetic  9.21 us (1%)
    psum x1, waiting for transfers between devices, shards(): grad_gate = lax.psum(weight_part, 'dp')  120 us
    psum x1, blocking collectives, shards(): parts_out = psum(conv_part, 'seq')  115 us
    all_to_all x2, blocking collectives, regroup(): lax.all_to_all(values, 'seq', split_axis=0, concat_axis=1, tiled=True)  86.7 us
    all_gather x1, waiting for transfers between devices, shards(): whole_gate = lax.all_gather(gate_weight, 'seq', axis=0, tiled=True)  68.7 us
    psum x1, blocking collectives, shards(): grad_conv = psum(parts_out, 'dp')  52.8 us
    all_to_all x1, blocking collectives, shards(): lax.all_to_all(d_monarch.reshape(local_blocks, block_size, feat_width), '...  42.4 us
    ppermute x2, waiting for transfers between devices, with_halo(): before = lax.ppermute(last, axis, up)  20.2 us
    unnamed x35, local copies, waits for them, and re-layouts  20 us
  transfers between devices with their start and end apart: 8, of which 4 were waited for; matrix products, arithmetic and copies ran while one was open for 4% of the time, Pallas kernels for 0%

profile of v1, /device:TPU:2, one launch (start us, length us, event | category | flops | bytes accessed | tf_op | source)
XLA Modules:
  0.0 636.2 jit_solution(4284799706685939097)
XLA Ops:
  7.9 68.7 %all-gather.2.cloned.1.call-done = bf16[1536,1536]{1,0:T(8,128)(2,1)} async-done(((bf16[48,1536]{1,0:T(8,128)(2,1)}), bf16[1536,1536]{1,0:T(8,128)(2,1)}) %all-gather.2.cloned.1.call-update) | async-done | bytes 4718608 | tf_op jit(solution)/shard_map/all_gather | solution.py:55
  76.6 7.6 %fusion.2 = (bf16[512,1536]{1,0:T(8,128)(2,1)S(1)}, f32[512,1536]{1,0:T(8,128)}) fusion(bf16[1,512,1536]{2,1,0:T(8,128)(2,1)} %param.7, bf16[1536,1536]{1,0:T(8,128)(2,1)} %all-gather.2.cloned.1.call-done, bf16[1,512,1536]{2,1,0:T(8,128)(2,1)} %param.6), kind=kOutput, calls=%fused_computation.9 | convolution fusion | flops 2418278400 | bytes 12582912 | tf_op jit(solution)/shard_map/dot_general | solution.py:56
  85.4 42.4 %all_to_all.63 = bf16[4,128,1536]{2,0,1:T(4,128)(2,1)S(1)} all-to-all(bf16[4,128,1536]{2,0,1:T(4,128)(2,1)S(1)} %copy.58), channel_id=1, replica_groups=mesh['seq'=32,'dp'=8] {'seq'}, dimensions={1} | all-to-all | bytes 3145728 | tf_op jit(solution)/shard_map/all_to_all | solution.py:62
  130.4 2.5 copy.61
  132.9 7.2 %all-to-all-start.3 = ((bf16[128,4,1536]{2,1,0:T(4,128)(2,1)}), bf16[128,4,1536]{2,1,0:T(4,128)(2,1)}, u32[]{:S(2)}, u32[]{:S(2)}) async-start(bf16[128,4,1536]{2,1,0:T(4,128)(2,1)} %copy.61), calls=%async_computation.3 | async-start | bytes 3145728 | tf_op jit(solution)/shard_map/all_to_all | solution.py:26
  143.0 6.2 collective-permute-start.1
  149.3 20.2 %collective-permute-done = bf16[1,1536]{1,0:T(2,128)(2,1)S(1)} collective-permute-done((bf16[1,1536]{1,0:T(2,128)(2,1)S(1)}, bf16[1,1536]{1,0:T(2,128)(2,1)S(1)}, u32[]{:S(2)}, u32[]{:S(2)}) %collective-permute-start) | collective-permute-done | bytes 3104 | tf_op jit(solution)/shard_map/ppermute | solution.py:15
  171.4 5.5 all-to-all-done.3
  176.9 3.1 copy.62
  180.0 3.7 all_to_all.58
  183.7 2.6 fusion.9
  191.1 43.9 %all_to_all.64 = bf16[128,4,1536]{2,1,0:T(4,128)(2,1)S(1)} all-to-all(bf16[128,4,1536]{2,1,0:T(4,128)(2,1)S(1)} %copy.53), channel_id=1, replica_groups=mesh['seq'=32,'dp'=8] {'seq'}, dimensions={0} | all-to-all | bytes 3145728 | tf_op jit(solution)/shard_map/all_to_all | solution.py:26
  239.2 42.8 %all_to_all.65 = bf16[128,4,1536]{2,1,0:T(4,128)(2,1)S(1)} all-to-all(bf16[128,4,1536]{2,1,0:T(4,128)(2,1)S(1)} %copy.56), channel_id=1, replica_groups=mesh['seq'=32,'dp'=8] {'seq'}, dimensions={0} | all-to-all | bytes 3145728 | tf_op jit(solution)/shard_map/all_to_all | solution.py:26
  284.9 9.2 %convolution_bitcast_fusion = f32[1536,1536]{0,1:T(8,128)} fusion(f32[1,512,1536]{2,1,0:T(8,128)} %reshape.55, bf16[1,512,1536]{2,1,0:T(8,128)(2,1)} %param.7, bf16[1,512,1536]{2,1,0:T(8,128)(2,1)} %param.6), kind=kOutput, calls=%fused_computation | convolution fusion | flops 2418278400 | bytes 15728640 | tf_op jit(solution)/shard_map/dot_general | solution.py:106
  294.1 9.6 %copy.70 = f32[1536,1536]{1,0:T(8,128)} copy(f32[1536,1536]{0,1:T(8,128)} %convolution_bitcast_fusion) | data formatting | bytes 18874368
  304.6 3.6 collective-permute-start.2
  308.3 4.7 collective-permute-start.3
  312.9 114.9 %psum.35 = f32[3,1536]{1,0:T(4,128)S(1)} all-reduce(f32[3,1536]{1,0:T(4,128)S(1)} %pad_maximum_fusion), channel_id=1, replica_groups=mesh['seq'=32,'dp'=8] {'seq'}, use_global_device_ids=true, to_apply=%region_3.0 | all-reduce | flops 4608 | bytes 36864 | tf_op jit(solution)/shard_map/psum | solution.py:115
  427.9 3.2 fusion.28
  431.1 52.8 %psum.36 = f32[3,1536]{1,0:T(4,128)} all-reduce(f32[3,1536]{1,0:T(4,128)S(1)} %psum.35), channel_id=1, replica_groups=mesh['seq'=32,'dp'=8] {'dp'}, use_global_device_ids=true, to_apply=%region_4.0 | all-reduce | flops 4608 | bytes 36864 | tf_op jit(solution)/shard_map/psum | solution.py:116
  483.9 3.7 maximum_convert_fusion.1
  491.2 2.3 copy.71
  493.5 9.8 %fusion.14 = bf16[1,512,1536]{2,1,0:T(8,128)(2,1)} fusion(bf16[1536,1536]{1,0:T(8,128)(2,1)} %all-gather.2.cloned.1.call-done, f32[514,1536]{1,0:T(8,128)} %maximum_convert_fusion.1, bf16[512,1536]{1,0:T(8,128)(2,1)S(1)} %bitcast.78, f32[512,1536]{1,0:T(8,128)} %reshape.52, bf16[1,512,1536]{2,1,0:T(8,128)(2,1)} %param.7, f32[1536]{0:T(1024)S(1)} %get-tuple-element.33, ...), kind=kOutput, calls=%fused_computation.31 | convolution fusion | flops 2424569856 | bytes 18892800 | tf_op jit(solution)/shard_map/dot_general | solution.py:101
  504.9 120.3 %all-reduce.3.cloned.1.call-done = (f32[48,1536]{0,1:T(8,128)}, f32[4,128,128]{2,1,0:T(8,128)}, f32[4,128,128]{2,1,0:T(8,128)}) async-done(((f32[48,1536]{0,1:T(8,128)}, f32[4,128,128]{2,1,0:T(8,128)}, f32[4,128,128]{2,1,0:T(8,128)}), (f32[48,1536]{0,1:T(8,128)}, f32[4,128,128]{2,1,0:T(8,128)}, f32[4,128,128]{2,1,0:T(8,128)})) %all-reduce.3.cloned.1.call-update) | async-done | bytes 819216 | tf_op jit(solution)/shard_map/psum | solution.py:114
  (67 shorter events, 31.7 us)
Async XLA Ops:
  7.2 176.5 %copy-start = (bf16[4,128,128]{2,1,0:T(8,128)(2,1)S(1)}, bf16[4,128,128]{2,1,0:T(8,128)(2,1)}, u32[]{:S(2)}) copy-start(bf16[4,128,128]{2,1,0:T(8,128)(2,1)} %param.10) | copy-start | bytes 393220
  7.2 69.4 %all-gather.2.cloned.1.call-start = ((), (), s32[]{:S(2)}) async-start(), calls=%async_computation.5 | async-start | bytes 4866048 | tf_op jit(solution)/shard_map/all_gather | solution.py:55
  127.8 1.9 copy-start.12
  128.6 1.1 copy-start.7
  132.9 16.3 %copy-start.14 = (f32[3,1536]{1,0:T(4,128)S(1)}, f32[3,1536]{1,0:T(4,128)}, u32[]{:S(2)}) copy-start(f32[3,1536]{1,0:T(4,128)} %param.8) | copy-start | bytes 55300
  132.9 44.0 %all-to-all-start.3 = ((bf16[128,4,1536]{2,1,0:T(4,128)(2,1)}), bf16[128,4,1536]{2,1,0:T(4,128)(2,1)}, u32[]{:S(2)}, u32[]{:S(2)}) async-start(bf16[128,4,1536]{2,1,0:T(4,128)(2,1)} %copy.61), calls=%async_computation.3 | async-start | bytes 3145728 | tf_op jit(solution)/shard_map/all_to_all | solution.py:26
  140.1 351.0 %reduce-scatter.4.cloned.1.call-start = ((), (), s32[]{:S(2)}) async-start(), calls=%async_computation.6 | async-start | bytes 9732096
  140.9 28.6 %collective-permute-start = (bf16[1,1536]{1,0:T(2,128)(2,1)S(1)}, bf16[1,1536]{1,0:T(2,128)(2,1)S(1)}, u32[]{:S(2)}, u32[]{:S(2)}) collective-permute-start(bf16[1,1536]{1,0:T(2,128)(2,1)S(1)} %get-tuple-element.41), channel_id=1, source_target_pairs={{0,8},{8,16},{16,24},{24,32},{32,40},{40,48},{48,56},{56,64},{64,7... | collective-permute-start | bytes 9224 | tf_op jit(solution)/shard_map/ppermute | solution.py:15
  143.0 26.5 %collective-permute-start.1 = (bf16[1,1536]{1,0:T(2,128)(2,1)S(1)}, bf16[1,1536]{1,0:T(2,128)(2,1)S(1)}, u32[]{:S(2)}, u32[]{:S(2)}) collective-permute-start(bf16[1,1536]{1,0:T(2,128)(2,1)S(1)} %get-tuple-element.42), channel_id=1, source_target_pairs={{8,0},{16,8},{24,16},{32,24},{40,32},{48,40},{56,48},{64,56},{72,6... | collective-permute-start | bytes 9224 | tf_op jit(solution)/shard_map/ppermute | solution.py:16
  183.7 2.6 copy-start.2
  186.3 1.6 copy-start.3
  187.9 1.1 copy-start.5
  235.9 1.2 copy-start.9
  303.8 321.3 %all-reduce.3.cloned.1.call-start = ((), (), s32[]{:S(2)}) async-start(), calls=%async_computation.7 | async-start | bytes 2621440 | tf_op jit(solution)/shard_map/psum | solution.py:114
  304.6 179.3 %collective-permute-start.2 = (bf16[1,1536]{1,0:T(2,128)(2,1)S(1)}, bf16[1,1536]{1,0:T(2,128)(2,1)S(1)}, u32[]{:S(2)}, u32[]{:S(2)}) collective-permute-start(bf16[1,1536]{1,0:T(2,128)(2,1)S(1)} %get-tuple-element.39), channel_id=1, source_target_pairs={{0,8},{8,16},{16,24},{24,32},{32,40},{40,48},{48,56},{56,64},{64,7... | collective-permute-start | bytes 9224 | tf_op jit(solution)/shard_map/ppermute | solution.py:15
  308.3 175.7 %collective-permute-start.3 = (bf16[1,1536]{1,0:T(2,128)(2,1)S(1)}, bf16[1,1536]{1,0:T(2,128)(2,1)S(1)}, u32[]{:S(2)}, u32[]{:S(2)}) collective-permute-start(bf16[1,1536]{1,0:T(2,128)(2,1)S(1)} %get-tuple-element.40), channel_id=1, source_target_pairs={{8,0},{16,8},{24,16},{32,24},{40,32},{48,40},{56,48},{64,56},{72,6... | collective-permute-start | bytes 9224 | tf_op jit(solution)/shard_map/ppermute | solution.py:16
  483.9 3.7 copy-start.8
  483.9 3.7 copy-start.10
  491.2 2.3 copy-start.4
  493.5 9.8 %copy-start.6 = (f32[512,1536]{1,0:T(8,128)S(1)}, f32[512,1536]{1,0:T(8,128)}, u32[]{:S(2)}) copy-start(f32[512,1536]{1,0:T(8,128)} %reshape.52) | copy-start | bytes 9437188
  493.5 9.8 %copy-start.11 = (f32[512,1536]{1,0:T(8,128)S(1)}, f32[512,1536]{1,0:T(8,128)}, u32[]{:S(2)}) copy-start(f32[512,1536]{1,0:T(8,128)} %get-tuple-element.44) | copy-start | bytes 9437188
  503.3 126.4 %copy-start.1 = (bf16[4,128,128]{2,1,0:T(8,128)(2,1)S(1)}, bf16[4,128,128]{2,1,0:T(8,128)(2,1)}, u32[]{:S(2)}) copy-start(bf16[4,128,128]{2,1,0:T(8,128)(2,1)} %param.10) | copy-start | bytes 393220
  625.1 3.8 copy-start.13
Sparse Core Ops, SparseCore 0:
  9.9 66.6 all-gather.1
  303.9 146.2 reduce-scatter.3
  493.6 131.4 all-reduce.2
